TPU v7x, 32 devices: a whole 2x2x4 slice. The times are simulated.
32 devices in a mesh: grp: 2 (over y), ia: 4 (over x, core), ja: 4 (over z).
Axes of the slice: x: 2, y: 2, z: 4, core: 2. Of those that a mesh axis runs over, the one named last changes fastest.
Arguments:
- amplitudes: float32 [16, 8, 160, 160], P(('grp', 'ia'), 'ja'), parts along dimension 0, may hold values from -3 to 3
- integrals: float32 [16, 8, 160, 160], P(('grp', 'ia'), 'ja'), parts along dimension 0, may hold values from -6 to 6
- row_intersection: float32 [16, 8, 8, 160, 160], P(('grp', 'ia'), 'ja'), parts along dimension 0, as said below
- column_intersection: float32 [16, 8, 8, 160, 160], P(('grp', 'ia'), 'ja'), parts along dimension 0, as said below
- row_tiles: int32 [16, 8], P(('grp', 'ia')), parts along dimension 0, may hold values from 0 to 7, as said below
- row_coupling: float32 [16, 8], P(('grp', 'ia')), parts along dimension 0, may hold values from 0.02 to 0.12
- row_counts: int32 [16], P(('grp', 'ia')), parts along dimension 0, may hold values from 1 to 8, as said below
- column_tiles: int32 [16, 8], P(('grp', 'ja')), parts along dimension 0, may hold values from 0 to 7, as said below
- column_coupling: float32 [16, 8], P(('grp', 'ja')), parts along dimension 0, may hold values from 0.02 to 0.12
- column_counts: int32 [16], P(('grp', 'ja')), parts along dimension 0, may hold values from 1 to 8, as said below
- virtual_energy: float32 [16, 8, 160], P(('grp', 'ia'), 'ja'), parts along dimension 0, may hold values from 0.5 to 3
- first_energy: float32 [16], P(('grp', 'ia')), parts along dimension 0, may hold values from -1.5 to -0.3
- second_energy: float32 [16], P(('grp', 'ja')), parts along dimension 0, may hold values from -1.5 to -0.3
Outputs:
- new_amplitudes: float32 [16, 8, 160, 160], P(('grp', 'ia'), 'ja'), parts along dimension 0
- last_residual: float32 [16, 8, 160, 160], P(('grp', 'ia'), 'ja'), parts along dimension 0
There are 2 independent parts, one for each index of `grp`. A program takes and returns all parts, laid end to end along the dimension named above; each array names one. Nothing has to cross between parts.
Inputs may be any that keep to these rules, and one draw needn't show every extreme that they name: `row_tiles`: each row holds 8 different first-fragment orbitals. `column_tiles`: each row holds 8 different second-fragment orbitals. `row_counts`: some orbital has all 8 slots live. `column_counts`: some orbital has all 8 slots live. `row_intersection`: identity plus an independent perturbation of full rank. `column_intersection`: identity plus an independent perturbation of full rank.
All inputs are finite; a program needn't handle non-finite values.
Results may differ from a plain program's by a relative error of at most 0.00017.
Values sent between devices are 32-bit elements; how exact they have to be, the bound alone decides.
No kernel may reach another device: no remote copies, remote signals or barrier semaphores. Data moves between devices by JAX's collectives and lax.ppermute only.
A program may use at most 128 MiB of HBM per device.

v0:
```python
import jax
import jax.numpy as jnp
from jax import lax
from jax.sharding import PartitionSpec as P

ITERS = 2


def sandwich(intersection, block):
    left = jnp.matmul(intersection, block, precision=lax.Precision.HIGHEST)
    return jnp.matmul(left, jnp.swapaxes(intersection, -1, -2), precision=lax.Precision.HIGHEST)


def coupled_sum(intersection, chosen, weight, counts, row_side):
    longest = jnp.max(counts)

    def one_slot(slot, total):
        over_slot = lax.dynamic_index_in_dim(intersection, slot, 2, keepdims=False)
        chosen_slot = lax.dynamic_index_in_dim(chosen, slot, 2, keepdims=False)
        weight_slot = lax.dynamic_index_in_dim(weight, slot, 1, keepdims=False)
        product = sandwich(over_slot, chosen_slot)
        if row_side:
            scaled = weight_slot[:, None, None, None] * product
        else:
            scaled = weight_slot[None, :, None, None] * product
        return total + scaled

    start = jnp.zeros(chosen.shape[:2] + chosen.shape[3:], jnp.float32)
    return lax.fori_loop(0, longest, one_slot, start)


def local(
    amplitudes,
    integrals,
    row_intersection,
    column_intersection,
    row_tiles,
    row_coupling,
    row_counts,
    column_tiles,
    column_coupling,
    column_counts,
    virtual_energy,
    first_energy,
    second_energy,
):
    denom = (
        virtual_energy[:, :, :, None]
        + virtual_energy[:, :, None, :]
        - first_energy[:, None, None, None]
        - second_energy[None, :, None, None]
    )
    slot_index = jnp.arange(row_tiles.shape[1], dtype=jnp.int32)
    row_weight = row_coupling * (slot_index[None, :] < row_counts[:, None]).astype(jnp.float32)
    column_weight = column_coupling * (slot_index[None, :] < column_counts[:, None]).astype(
        jnp.float32
    )
    current = amplitudes
    residual = jnp.zeros_like(amplitudes)
    for iteration in range(ITERS):
        gathered_rows = lax.all_gather(current, "ia", axis=0, tiled=True)
        gathered_columns = lax.all_gather(current, "ja", axis=1, tiled=True)
        row_chosen = jnp.swapaxes(gathered_rows[row_tiles], 1, 2)
        column_chosen = gathered_columns[:, column_tiles]
        row_term = coupled_sum(row_intersection, row_chosen, row_weight, row_counts, True)
        column_term = coupled_sum(
            column_intersection, column_chosen, column_weight, column_counts, False
        )
        residual = integrals + denom * current - row_term - column_term
        current = current - residual / denom
    return (current, residual)


def solution(mesh):
    placed = (
        P(("grp", "ia"), "ja", None, None),
        P(("grp", "ia"), "ja", None, None),
        P(("grp", "ia"), "ja", None, None, None),
        P(("grp", "ia"), "ja", None, None, None),
        P(("grp", "ia"), None),
        P(("grp", "ia"), None),
        P(("grp", "ia")),
        P(("grp", "ja"), None),
        P(("grp", "ja"), None),
        P(("grp", "ja")),
        P(("grp", "ia"), "ja", None),
        P(("grp", "ia")),
        P(("grp", "ja")),
    )
    return jax.shard_map(
        local,
        mesh=mesh,
        in_specs=placed,
        out_specs=(P(("grp", "ia"), "ja", None, None), P(("grp", "ia"), "ja", None, None)),
        check_vma=False,
    )
```

profile of v0, /device:TPU:16, one launch (start us, length us, event | category | flops | bytes accessed | tf_op | source)
XLA Modules:
  0.0 275.3 jit_solution(13624956626482143141)
XLA Ops:
  9.5 5.4 %copy.44 = f32[2,2,8,160,160]{4,3,1,0,2:T(8,128)} copy(f32[2,2,8,160,160]{4,3,2,1,0:T(8,128)} %param.23) | data formatting | bytes 6553600 | tf_op jit(solution)/shard_map/while | solution.py:29
  15.1 5.6 %copy.47 = f32[2,2,8,160,160]{4,3,1,0,2:T(8,128)} copy(f32[2,2,8,160,160]{4,3,2,1,0:T(8,128)} %param.24) | data formatting | bytes 6553600 | tf_op jit(solution)/shard_map/while | solution.py:29
  22.1 14.0 %all-gather.5.cloned.1.call-done = f32[8,2,160,160]{3,2,1,0:T(8,128)} async-done(((f32[2,2,160,160]{3,2,1,0:T(8,128)}), f32[8,2,160,160]{3,2,1,0:T(8,128)}) %all-gather.5.cloned.1.call-update) | async-done | bytes 1638416 | tf_op jit(solution)/shard_map/all_gather | solution.py:61
  36.2 5.0 %gather_fusion = f32[16,2,160,160]{3,2,1,0:T(8,128)} fusion(f32[8,2,160,160]{3,2,1,0:T(8,128)} %all-gather.5.cloned.1.call-done, s32[1024]{0:T(1024)S(1)} %pad_clamp_fusion.1), kind=kCustom, calls=%fused_computation | custom fusion | bytes 6553664 | tf_op jit(solution)/shard_map/gather | solution.py:63
  41.2 34.7 %while.40 = (s32[]{:T(128)}, f32[2,2,160,160]{3,2,1,0:T(8,128)S(1)}, s32[]{:T(128)}, f32[2,8]{0,1:T(8,128)S(1)}, f32[2,2,8,160,160]{4,3,1,0,2:T(8,128)}, /*index...) while((s32[]{:T(128)}, f32[2,2,160,160]{3,2,1,0:T(8,128)S(1)}, s32[]{:T(128)}, ...), condition=%wide.region_2.3_spmd, body=%wide.region_1.2_spmd.sunk | while | flops 393420800 | bytes 3605663 | solution.py:29
  44.0 2.1 fusion.81
  46.8 2.1 fusion.79
  56.5 2.1 fusion.79
  63.5 2.1 fusion.81
  71.1 2.1 fusion.79
  75.9 15.4 %all-gather.7.cloned.1.call-done = f32[2,8,160,160]{3,2,1,0:T(8,128)} async-done(((f32[2,2,160,160]{3,2,1,0:T(8,128)}), f32[2,8,160,160]{3,2,1,0:T(8,128)}) %all-gather.7.cloned.1.call-update) | async-done | bytes 1638416 | tf_op jit(solution)/shard_map/all_gather | solution.py:62
  91.3 5.0 %gather_fusion.1 = f32[16,2,160,160]{3,2,1,0:T(8,128)} fusion(f32[2,8,160,160]{3,2,1,0:T(8,128)} %all-gather.7.cloned.1.call-done, s32[1024]{0:T(1024)S(1)} %pad_clamp_fusion), kind=kCustom, calls=%fused_computation.1 | custom fusion | bytes 6553664 | tf_op jit(solution)/shard_map/gather | solution.py:64
  96.4 39.2 %while.41 = (s32[]{:T(128)}, f32[2,2,160,160]{3,2,1,0:T(8,128)S(1)}, s32[]{:T(128)}, f32[2,8]{0,1:T(8,128)S(1)}, f32[2,2,8,160,160]{4,3,1,0,2:T(8,128)}, /*index...) while((s32[]{:T(128)}, f32[2,2,160,160]{3,2,1,0:T(8,128)S(1)}, s32[]{:T(128)}, ...), condition=%wide.region_5.6_spmd, body=%wide.region_4.5_spmd.sunk | while | flops 393420800 | bytes 3605663 | solution.py:29
  137.3 25.0 %all-gather.9.cloned.1.call-done = f32[8,2,160,160]{3,2,1,0:T(8,128)} async-done(((f32[2,2,160,160]{3,2,1,0:T(8,128)}), f32[8,2,160,160]{3,2,1,0:T(8,128)}) %all-gather.9.cloned.1.call-update) | async-done | bytes 1638416 | tf_op jit(solution)/shard_map/all_gather | solution.py:61
  162.3 4.9 %gather_fusion.2 = f32[16,2,160,160]{3,2,1,0:T(8,128)} fusion(f32[8,2,160,160]{3,2,1,0:T(8,128)} %all-gather.9.cloned.1.call-done, s32[1024]{0:T(1024)S(1)} %pad_clamp_fusion.1), kind=kCustom, calls=%fused_computation.2 | custom fusion | bytes 6553664 | tf_op jit(solution)/shard_map/gather | solution.py:63
  167.2 5.4 %copy.60 = f32[2,8,2,160,160]{4,3,2,0,1:T(8,128)} copy(f32[2,8,2,160,160]{4,3,2,1,0:T(8,128)} %bitcast.100) | data formatting | bytes 6553600 | tf_op jit(solution)/shard_map/gather | solution.py:63
  172.6 34.7 %while.42 = (s32[]{:T(128)}, f32[2,2,160,160]{3,2,1,0:T(8,128)S(1)}, s32[]{:T(128)}, f32[2,8]{0,1:T(8,128)S(1)}, f32[2,2,8,160,160]{4,3,1,0,2:T(8,128)}, /*index...) while((s32[]{:T(128)}, f32[2,2,160,160]{3,2,1,0:T(8,128)S(1)}, s32[]{:T(128)}, ...), condition=%wide.region_7.8_spmd, body=%wide.region_6.7_spmd.sunk | while | flops 393420800 | bytes 3605663 | solution.py:29
  173.3 2.1 fusion.92
  183.1 2.1 fusion.92
  197.6 2.1 fusion.92
  207.3 10.6 %all-gather.11.cloned.1.call-done = f32[2,8,160,160]{3,2,1,0:T(8,128)} async-done(((f32[2,2,160,160]{3,2,1,0:T(8,128)}), f32[2,8,160,160]{3,2,1,0:T(8,128)}) %all-gather.11.cloned.1.call-update) | async-done | bytes 1638416 | tf_op jit(solution)/shard_map/all_gather | solution.py:62
  217.9 5.0 %gather_fusion.3 = f32[16,2,160,160]{3,2,1,0:T(8,128)} fusion(f32[2,8,160,160]{3,2,1,0:T(8,128)} %all-gather.11.cloned.1.call-done, s32[1024]{0:T(1024)S(1)} %pad_clamp_fusion), kind=kCustom, calls=%fused_computation.3 | custom fusion | bytes 6553664 | tf_op jit(solution)/shard_map/gather | solution.py:64
  222.8 5.4 %copy.59 = f32[2,8,2,160,160]{4,3,0,2,1:T(8,128)} copy(f32[2,8,2,160,160]{4,3,2,1,0:T(8,128)} %bitcast.101) | data formatting | bytes 6553600 | tf_op jit(solution)/shard_map/gather | solution.py:64
  228.3 39.1 %while.43 = (s32[]{:T(128)}, f32[2,2,160,160]{3,2,1,0:T(8,128)S(1)}, s32[]{:T(128)}, f32[2,8]{0,1:T(8,128)S(1)}, f32[2,2,8,160,160]{4,3,1,0,2:T(8,128)}, /*index...) while((s32[]{:T(128)}, f32[2,2,160,160]{3,2,1,0:T(8,128)S(1)}, s32[]{:T(128)}, ...), condition=%wide.region_9.10_spmd, body=%wide.region_8.9_spmd.sunk | while | flops 393420800 | bytes 3605663 | solution.py:29
  (130 shorter events, 114.2 us)
Async XLA Ops:
  7.2 29.0 %all-gather.5.cloned.1.call-start = ((), (), s32[]{:S(2)}) async-start(), calls=%async_computation | async-start | bytes 3276800 | tf_op jit(solution)/shard_map/all_gather | solution.py:61
  7.9 83.4 %all-gather.7.cloned.1.call-start = ((), (), s32[]{:S(2)}) async-start(), calls=%async_computation.1 | async-start | bytes 3276800 | tf_op jit(solution)/shard_map/all_gather | solution.py:62
  8.6 153.7 %all-gather.9.cloned.1.call-start = ((), (), s32[]{:S(2)}) async-start(), calls=%async_computation.2 | async-start | bytes 3276800 | tf_op jit(solution)/shard_map/all_gather | solution.py:61
  9.5 5.4 %copy-start.6 = (f32[2,8]{1,0:T(2,128)S(1)}, f32[2,8]{1,0:T(2,128)}, u32[]{:S(2)}) copy-start(f32[2,8]{1,0:T(2,128)} %param.26) | copy-start | bytes 196
  9.5 5.5 %copy-start.8 = (s32[2,8]{1,0:T(2,128)S(1)}, s32[2,8]{1,0:T(2,128)}, u32[]{:S(2)}) copy-start(s32[2,8]{1,0:T(2,128)} %param.28) | copy-start | bytes 196
  15.1 5.6 %copy-start.7 = (f32[2,8]{1,0:T(2,128)S(1)}, f32[2,8]{1,0:T(2,128)}, u32[]{:S(2)}) copy-start(f32[2,8]{1,0:T(2,128)} %param.29) | copy-start | bytes 196
  15.1 5.7 %copy-start.9 = (s32[2]{0:T(128)S(1)}, s32[2]{0:T(128)}, u32[]{:S(2)}) copy-start(s32[2]{0:T(128)} %param.27) | copy-start | bytes 28
  15.1 6.4 %copy-start.10 = (s32[2]{0:T(128)S(1)}, s32[2]{0:T(128)}, u32[]{:S(2)}) copy-start(s32[2]{0:T(128)} %param.30) | copy-start | bytes 28
  96.3 39.2 %copy-start.1 = (f32[2,2,160,160]{3,2,1,0:T(8,128)S(1)}, f32[2,2,160,160]{3,2,1,0:T(8,128)}, u32[]{:S(2)}) copy-start(f32[2,2,160,160]{3,2,1,0:T(8,128)} %param.21) | copy-start | bytes 1228804
  96.3 39.2 %copy-start.2 = (f32[2,2,160,160]{3,2,1,0:T(8,128)S(1)}, f32[2,2,160,160]{3,2,1,0:T(8,128)}, u32[]{:S(2)}) copy-start(f32[2,2,160,160]{3,2,1,0:T(8,128)} %param.22) | copy-start | bytes 1228804
  96.3 39.2 %copy-start.3 = (f32[2,2,160]{2,1,0:T(2,128)S(1)}, f32[2,2,160]{2,1,0:T(2,128)}, u32[]{:S(2)}) copy-start(f32[2,2,160]{2,1,0:T(2,128)} %param.31) | copy-start | bytes 7684
  96.4 39.2 %copy-start.4 = (f32[2]{0:T(128)S(1)}, f32[2]{0:T(128)}, u32[]{:S(2)}) copy-start(f32[2]{0:T(128)} %param.33) | copy-start | bytes 28
  96.4 39.2 %copy-start.5 = (f32[2]{0:T(128)S(1)}, f32[2]{0:T(128)}, u32[]{:S(2)}) copy-start(f32[2]{0:T(128)} %param.32) | copy-start | bytes 28
  136.8 81.1 %all-gather.11.cloned.1.call-start = ((), (), s32[]{:S(2)}) async-start(), calls=%async_computation.3 | async-start | bytes 3276800 | tf_op jit(solution)/shard_map/all_gather | solution.py:62
  228.3 39.2 %copy-start = (f32[2,2,160,160]{3,2,1,0:T(8,128)S(1)}, f32[2,2,160,160]{3,2,1,0:T(8,128)}, u32[]{:S(2)}) copy-start(f32[2,2,160,160]{3,2,1,0:T(8,128)} %divide_subtract_fusion.1) | copy-start | bytes 1228804
Sparse Core Ops, SparseCore 0:
  9.5 26.5 all-gather.4
  37.7 53.5 all-gather.6
  136.9 25.3 all-gather.8
  164.3 53.5 all-gather.10
where the time goes:
time: 278 us; the launch traced here: 275 us
  matrix products  123 us (44%)
  waiting for transfers between devices  66.9 us (24%)
  local copies, waits for them, and re-layouts  42.4 us (15%)
  loops' own time  24 us (9%)
  between operations  14 us (5%)
  other arithmetic  4.52 us (2%)
    dot_general x30, matrix products, sandwich(): left = jnp.matmul(intersection, block, precision=lax.Precision.HIGHEST)  61.7 us
    dot_general x30, matrix products, sandwich(): jnp.matmul(left, jnp.swapaxes(intersection, -1, -2), precision=lax.Precis...  61.7 us
    all_gather x2, waiting for transfers between devices, local(): gathered_rows = lax.all_gather(current, 'ia', axis=0, tiled=True)  39 us
    all_gather x2, waiting for transfers between devices, local(): gathered_columns = lax.all_gather(current, 'ja', axis=1, tiled=True)  26 us
    another operation x4, loops' own time, coupled_sum(): return lax.fori_loop(0, longest, one_slot, start)  24 us
    gather x3, local copies, waits for them, and re-layouts, local(): column_chosen = gathered_columns[:, column_tiles]  15.3 us
    gather x3, local copies, waits for them, and re-layouts, local(): row_chosen = jnp.swapaxes(gathered_rows[row_tiles], 1, 2)  15.2 us
    while x2, local copies, waits for them, and re-layouts, coupled_sum(): return lax.fori_loop(0, longest, one_slot, start)  11 us
  transfers between devices with their start and end apart: 4, of which 4 were waited for; matrix products, arithmetic and copies ran while one was open for 31% of the time, Pallas kernels for 0%

commit v1 on v0

--- a/solution.py
+++ b/solution.py
@@ -4,6 +4,22 @@
 from jax.sharding import PartitionSpec as P
 
 ITERS = 2
+
+
+def ring_gather(x, axis, dim):
+    ways, here, lap = (lax.axis_size(axis), lax.axis_index(axis), x.shape[dim])
+    dims = [n * ways if d == dim else n for d, n in enumerate(x.shape)]
+    full = lax.dynamic_update_slice_in_dim(jnp.zeros(dims, x.dtype), x, here * lap, axis=dim)
+    going_up = going_down = x
+    for far in range(1, ways // 2 + 1):
+        going_up = lax.ppermute(going_up, axis, [(d, (d + 1) % ways) for d in range(ways)])
+        full = lax.dynamic_update_slice_in_dim(full, going_up, (here - far) % ways * lap, axis=dim)
+        if 2 * far < ways:
+            going_down = lax.ppermute(going_down, axis, [(d, (d - 1) % ways) for d in range(ways)])
+            full = lax.dynamic_update_slice_in_dim(
+                full, going_down, (here + far) % ways * lap, axis=dim
+            )
+    return full
 
 
 def sandwich(intersection, block):
@@ -59,7 +75,7 @@
     residual = jnp.zeros_like(amplitudes)
     for iteration in range(ITERS):
         gathered_rows = lax.all_gather(current, "ia", axis=0, tiled=True)
-        gathered_columns = lax.all_gather(current, "ja", axis=1, tiled=True)
+        gathered_columns = ring_gather(current, "ja", 1)
         row_chosen = jnp.swapaxes(gathered_rows[row_tiles], 1, 2)
         column_chosen = gathered_columns[:, column_tiles]
         row_term = coupled_sum(row_intersection, row_chosen, row_weight, row_counts, True)

time: 278 us -> 297 us (1.068)
  the two profiles are of different devices: /device:TPU:16 before, /device:TPU:19 now
where the time goes in v1:
time: 297 us; the launch traced here: 294 us
  matrix products  131 us (44%)
  waiting for transfers between devices  56.8 us (19%)
  local copies, waits for them, and re-layouts  55.4 us (19%)
  loops' own time  25.5 us (9%)
  between operations  14.3 us (5%)
  other arithmetic  6.34 us (2%)
  starting transfers between devices  4.47 us (2%)
    dot_general x32, matrix products, sandwich(): jnp.matmul(left, jnp.swapaxes(intersection, -1, -2), precision=lax.Precis...  65.7 us
    dot_general x32, matrix products, sandwich(): left = jnp.matmul(intersection, block, precision=lax.Precision.HIGHEST)  65.6 us
    ppermute x4, waiting for transfers between devices, ring_gather(): lax.ppermute(going_up, axis, [(d, (d + 1) % ways) for d in range(ways)])  56.7 us
    another operation x4, loops' own time, coupled_sum(): return lax.fori_loop(0, longest, one_slot, start)  25.5 us
    gather x4, local copies, waits for them, and re-layouts, local(): column_chosen = gathered_columns[:, column_tiles]  18.8 us
    gather x3, local copies, waits for them, and re-layouts, local(): row_chosen = jnp.swapaxes(gathered_rows[row_tiles], 1, 2)  15.3 us
    while x2, local copies, waits for them, and re-layouts, coupled_sum(): return lax.fori_loop(0, longest, one_slot, start)  10.8 us
  transfers between devices with their start and end apart: 8, of which 4 were waited for; matrix products, arithmetic and copies ran while one was open for 37% of the time, Pallas kernels for 0%

profile of v1, /device:TPU:19, one launch (start us, length us, event | category | flops | bytes accessed | tf_op | source)
XLA Modules:
  0.0 294.2 jit_solution(18247868047478618065)
XLA Ops:
  13.8 9.5 %collective-permute-done = f32[2,2,160,160]{3,2,1,0:T(8,128)S(1)} collective-permute-done((f32[2,2,160,160]{3,2,1,0:T(8,128)}, f32[2,2,160,160]{3,2,1,0:T(8,128)S(1)}, u32[]{:S(2)}, u32[]{:S(2)}) %collective-permute-start) | collective-permute-done | bytes 409632 | tf_op jit(solution)/shard_map/ppermute | solution.py:15
  27.5 5.4 %copy.37 = f32[2,2,8,160,160]{4,3,1,0,2:T(8,128)} copy(f32[2,2,8,160,160]{4,3,2,1,0:T(8,128)} %param.24) | data formatting | bytes 6553600 | tf_op jit(solution)/shard_map/while | solution.py:45
  32.9 5.4 %copy.33 = f32[2,2,8,160,160]{4,3,1,0,2:T(8,128)} copy(f32[2,2,8,160,160]{4,3,2,1,0:T(8,128)} %param.23) | data formatting | bytes 6553600 | tf_op jit(solution)/shard_map/while | solution.py:45
  39.5 10.4 %collective-permute-done.2 = f32[2,2,160,160]{3,2,1,0:T(8,128)} collective-permute-done((f32[2,2,160,160]{3,2,1,0:T(8,128)S(1)}, f32[2,2,160,160]{3,2,1,0:T(8,128)}, u32[]{:S(2)}, u32[]{:S(2)}) %collective-permute-start.2) | collective-permute-done | bytes 409632 | tf_op jit(solution)/shard_map/ppermute | solution.py:15
  51.0 3.1 %gather_fusion.1 = f32[16,2,160,160]{3,2,1,0:T(8,128)} fusion(f32[2,8,160,160]{3,2,1,0:T(8,128)S(1)} %constant_dynamic-update-slice_fusion.4, s32[1024]{0:T(1024)S(1)} %pad_clamp_fusion), kind=kCustom, calls=%fused_computation.1 | custom fusion | bytes 6553664 | tf_op jit(solution)/shard_map/gather | solution.py:80
  54.2 5.4 %copy.48 = f32[2,8,2,160,160]{4,3,0,2,1:T(8,128)} copy(f32[2,8,2,160,160]{4,3,2,1,0:T(8,128)} %bitcast.103) | data formatting | bytes 6553600 | tf_op jit(solution)/shard_map/gather | solution.py:80
  59.6 39.1 %while.41 = (s32[]{:T(128)}, f32[2,2,160,160]{3,2,1,0:T(8,128)S(1)}, s32[]{:T(128)}, f32[2,8]{0,1:T(8,128)S(1)}, f32[2,2,8,160,160]{4,3,1,0,2:T(8,128)}, /*index...) while((s32[]{:T(128)}, f32[2,2,160,160]{3,2,1,0:T(8,128)S(1)}, s32[]{:T(128)}, ...), condition=%wide.region_5.6_spmd, body=%wide.region_4.5_spmd.sunk | while | flops 393420800 | bytes 3605663 | solution.py:45
  62.4 2.1 fusion.91
  67.2 2.1 fusion.91
  86.4 2.1 fusion.91
  98.7 5.0 %gather_fusion = f32[16,2,160,160]{3,2,1,0:T(8,128)} fusion(f32[8,2,160,160]{3,2,1,0:T(8,128)} %all-gather.3.cloned.1.call-done, s32[1024]{0:T(1024)S(1)} %pad_clamp_fusion.1), kind=kCustom, calls=%fused_computation | custom fusion | bytes 6553664 | tf_op jit(solution)/shard_map/gather | solution.py:79
  103.8 39.5 %while.40 = (s32[]{:T(128)}, f32[2,2,160,160]{3,2,1,0:T(8,128)S(1)}, s32[]{:T(128)}, f32[2,8]{0,1:T(8,128)S(1)}, f32[2,2,8,160,160]{4,3,1,0,2:T(8,128)}, /*index...) while((s32[]{:T(128)}, f32[2,2,160,160]{3,2,1,0:T(8,128)S(1)}, s32[]{:T(128)}, ...), condition=%wide.region_2.3_spmd, body=%wide.region_1.2_spmd.sunk | while | flops 393420800 | bytes 3605663 | solution.py:45
  116.4 2.1 fusion.84
  147.0 24.2 %collective-permute-done.3 = f32[2,2,160,160]{3,2,1,0:T(8,128)S(1)} collective-permute-done((f32[2,2,160,160]{3,2,1,0:T(8,128)S(1)}, f32[2,2,160,160]{3,2,1,0:T(8,128)S(1)}, u32[]{:S(2)}, u32[]{:S(2)}) %collective-permute-start.3) | collective-permute-done | bytes 409632 | tf_op jit(solution)/shard_map/ppermute | solution.py:15
  173.0 12.7 %collective-permute-done.5 = f32[2,2,160,160]{3,2,1,0:T(8,128)S(1)} collective-permute-done((f32[2,2,160,160]{3,2,1,0:T(8,128)S(1)}, f32[2,2,160,160]{3,2,1,0:T(8,128)S(1)}, u32[]{:S(2)}, u32[]{:S(2)}) %collective-permute-start.5) | collective-permute-done | bytes 409632 | tf_op jit(solution)/shard_map/ppermute | solution.py:15
  186.6 4.9 %gather_fusion.3 = f32[16,2,160,160]{3,2,1,0:T(8,128)} fusion(f32[2,8,160,160]{3,2,1,0:T(8,128)} %constant_dynamic-update-slice_fusion, s32[1024]{0:T(1024)S(1)} %pad_clamp_fusion), kind=kCustom, calls=%fused_computation.3 | custom fusion | bytes 6553664 | tf_op jit(solution)/shard_map/gather | solution.py:80
  191.4 5.4 %copy.46 = f32[2,8,2,160,160]{4,3,0,2,1:T(8,128)} copy(f32[2,8,2,160,160]{4,3,2,1,0:T(8,128)} %bitcast.101) | data formatting | bytes 6553600 | tf_op jit(solution)/shard_map/gather | solution.py:80
  196.9 39.1 %while.43 = (s32[]{:T(128)}, f32[2,2,160,160]{3,2,1,0:T(8,128)S(1)}, s32[]{:T(128)}, f32[2,8]{0,1:T(8,128)S(1)}, f32[2,2,8,160,160]{4,3,1,0,2:T(8,128)}, /*index...) while((s32[]{:T(128)}, f32[2,2,160,160]{3,2,1,0:T(8,128)S(1)}, s32[]{:T(128)}, ...), condition=%wide.region_9.10_spmd, body=%wide.region_8.9_spmd.sunk | while | flops 393420800 | bytes 3605663 | solution.py:45
  218.9 2.1 fusion.105
  236.0 5.0 %gather_fusion.2 = f32[16,2,160,160]{3,2,1,0:T(8,128)} fusion(f32[8,2,160,160]{3,2,1,0:T(8,128)} %all-gather.5.cloned.1.call-done, s32[1024]{0:T(1024)S(1)} %pad_clamp_fusion.1), kind=kCustom, calls=%fused_computation.2 | custom fusion | bytes 6553664 | tf_op jit(solution)/shard_map/gather | solution.py:79
  241.0 5.4 %copy.47 = f32[2,8,2,160,160]{4,3,2,0,1:T(8,128)} copy(f32[2,8,2,160,160]{4,3,2,1,0:T(8,128)} %bitcast.102) | data formatting | bytes 6553600 | tf_op jit(solution)/shard_map/gather | solution.py:79
  246.5 39.5 %while.42 = (s32[]{:T(128)}, f32[2,2,160,160]{3,2,1,0:T(8,128)S(1)}, s32[]{:T(128)}, f32[2,8]{0,1:T(8,128)S(1)}, f32[2,2,8,160,160]{4,3,1,0,2:T(8,128)}, /*index...) while((s32[]{:T(128)}, f32[2,2,160,160]{3,2,1,0:T(8,128)S(1)}, s32[]{:T(128)}, ...), condition=%wide.region_7.8_spmd, body=%wide.region_6.7_spmd.sunk | while | flops 393420800 | bytes 3605663 | solution.py:45
  254.2 2.1 fusion.98
  273.5 2.1 fusion.98
  (145 shorter events, 138.3 us)
Async XLA Ops:
  7.2 91.6 %all-gather.3.cloned.1.call-start = ((), (), s32[]{:S(2)}) async-start(), calls=%async_computation | async-start | bytes 3276800 | tf_op jit(solution)/shard_map/all_gather | solution.py:77
  7.2 16.1 %collective-permute-start = (f32[2,2,160,160]{3,2,1,0:T(8,128)}, f32[2,2,160,160]{3,2,1,0:T(8,128)S(1)}, u32[]{:S(2)}, u32[]{:S(2)}) collective-permute-start(f32[2,2,160,160]{3,2,1,0:T(8,128)} %param.21), channel_id=1, source_target_pairs={{0,1},{1,2},{2,3},{3,0},{4,5},{5,6},{6,7},{7,4},{8,9},{9,10},{10,1... | collective-permute-start | bytes 1228808 | tf_op jit(solution)/shard_map/ppermute | solution.py:15
  8.6 29.8 %collective-permute-start.1 = (f32[2,2,160,160]{3,2,1,0:T(8,128)}, f32[2,2,160,160]{3,2,1,0:T(8,128)}, u32[]{:S(2)}, u32[]{:S(2)}) collective-permute-start(f32[2,2,160,160]{3,2,1,0:T(8,128)} %param.21), channel_id=1, source_target_pairs={{0,3},{1,0},{2,1},{3,2},{4,7},{5,4},{6,5},{7,6},{8,11},{9,8},{10,9... | collective-permute-start | bytes 1228808 | tf_op jit(solution)/shard_map/ppermute | solution.py:18
  8.8 227.3 %all-gather.5.cloned.1.call-start = ((), (), s32[]{:S(2)}) async-start(), calls=%async_computation.1 | async-start | bytes 3276800 | tf_op jit(solution)/shard_map/all_gather | solution.py:77
  23.3 26.6 %collective-permute-start.2 = (f32[2,2,160,160]{3,2,1,0:T(8,128)S(1)}, f32[2,2,160,160]{3,2,1,0:T(8,128)}, u32[]{:S(2)}, u32[]{:S(2)}) collective-permute-start(f32[2,2,160,160]{3,2,1,0:T(8,128)S(1)} %collective-permute-done), channel_id=1, source_target_pairs={{0,1},{1,2},{2,3},{3,0},{4,5},{5,6},{6,7},{7,4},{8,9},{9,10},{10,1... | collective-permute-start | bytes 1228808 | tf_op jit(solution)/shard_map/ppermute | solution.py:15
  103.8 39.9 %copy-start.1 = (f32[2,2,160,160]{3,2,1,0:T(8,128)S(1)}, f32[2,2,160,160]{3,2,1,0:T(8,128)}, u32[]{:S(2)}) copy-start(f32[2,2,160,160]{3,2,1,0:T(8,128)} %param.21) | copy-start | bytes 1228804
  103.8 39.9 %copy-start.4 = (f32[2,2,160,160]{3,2,1,0:T(8,128)S(1)}, f32[2,2,160,160]{3,2,1,0:T(8,128)}, u32[]{:S(2)}) copy-start(f32[2,2,160,160]{3,2,1,0:T(8,128)} %param.22) | copy-start | bytes 1228804
  103.8 39.9 %copy-start.5 = (f32[2,2,160]{2,1,0:T(2,128)S(1)}, f32[2,2,160]{2,1,0:T(2,128)}, u32[]{:S(2)}) copy-start(f32[2,2,160]{2,1,0:T(2,128)} %param.31) | copy-start | bytes 7684
  103.8 39.9 %copy-start.6 = (f32[2]{0:T(128)S(1)}, f32[2]{0:T(128)}, u32[]{:S(2)}) copy-start(f32[2]{0:T(128)} %param.33) | copy-start | bytes 28
  103.8 39.8 %copy-start.7 = (f32[2]{0:T(128)S(1)}, f32[2]{0:T(128)}, u32[]{:S(2)}) copy-start(f32[2]{0:T(128)} %param.32) | copy-start | bytes 28
  144.0 1.6 copy-start
  145.6 25.6 %copy-start.2 = (f32[2,2,160,160]{3,2,1,0:T(8,128)}, f32[2,2,160,160]{3,2,1,0:T(8,128)S(1)}, u32[]{:S(2)}) copy-start(f32[2,2,160,160]{3,2,1,0:T(8,128)S(1)} %get-tuple-element.261) | copy-start | bytes 1228804
  145.6 25.6 %collective-permute-start.3 = (f32[2,2,160,160]{3,2,1,0:T(8,128)S(1)}, f32[2,2,160,160]{3,2,1,0:T(8,128)S(1)}, u32[]{:S(2)}, u32[]{:S(2)}) collective-permute-start(f32[2,2,160,160]{3,2,1,0:T(8,128)S(1)} %get-tuple-element.261), channel_id=1, source_target_pairs={{0,1},{1,2},{2,3},{3,0},{4,5},{5,6},{6,7},{7,4},{8,9},{9,10},{10,1... | collective-permute-start | bytes 1228808 | tf_op jit(solution)/shard_map/ppermute | solution.py:15
  145.6 26.5 %collective-permute-start.4 = (f32[2,2,160,160]{3,2,1,0:T(8,128)S(1)}, f32[2,2,160,160]{3,2,1,0:T(8,128)S(1)}, u32[]{:S(2)}, u32[]{:S(2)}) collective-permute-start(f32[2,2,160,160]{3,2,1,0:T(8,128)S(1)} %get-tuple-element.261), channel_id=1, source_target_pairs={{0,3},{1,0},{2,1},{3,2},{4,7},{5,4},{6,5},{7,6},{8,11},{9,8},{10,9... | collective-permute-start | bytes 1228808 | tf_op jit(solution)/shard_map/ppermute | solution.py:18
  171.2 14.5 %collective-permute-start.5 = (f32[2,2,160,160]{3,2,1,0:T(8,128)S(1)}, f32[2,2,160,160]{3,2,1,0:T(8,128)S(1)}, u32[]{:S(2)}, u32[]{:S(2)}) collective-permute-start(f32[2,2,160,160]{3,2,1,0:T(8,128)S(1)} %collective-permute-done.3), channel_id=1, source_target_pairs={{0,1},{1,2},{2,3},{3,0},{4,5},{5,6},{6,7},{7,4},{8,9},{9,10},{10,1... | collective-permute-start | bytes 1228808 | tf_op jit(solution)/shard_map/ppermute | solution.py:15
  246.5 39.5 %copy-start.3 = (f32[2,2,160,160]{3,2,1,0:T(8,128)S(1)}, f32[2,2,160,160]{3,2,1,0:T(8,128)}, u32[]{:S(2)}) copy-start(f32[2,2,160,160]{3,2,1,0:T(8,128)} %copy-done.2) | copy-start | bytes 1228804
Sparse Core Ops, SparseCore 0:
  9.5 26.0 all-gather.2
  171.4 23.8 all-gather.4
